TPU v7x, 128 devices: a whole 4x4x4 slice. The times are simulated.
128 devices in a mesh: tile: 16 (over x, z_lo, core), col: 8 (over y, z_hi).
Axes of the slice: x: 4, y: 4, z: 4 (z_hi: 2, z_lo: 2; z = z_hi * 2 + z_lo), core: 2. Of those that a mesh axis runs over, the one named last changes fastest.
Arguments:
- u_velocity: float32 [8192, 4096], P('tile', 'col'), may hold values from -12 to 12
- v_velocity: float32 [8192, 4096], P('tile', 'col'), may hold values from -12 to 12
- ocean_mask: int32 [64, 32], P('tile', 'col'), may hold values from 0 to 1, as said below
- tile_owner: int32 [64, 32], P('tile', 'col'), may hold values from 0 to 15, as said below
- lower_edge_quarter_turns: int32 [16], replicated, may hold values from 0 to 3
Outputs:
- library: float32 [16, 8, 16, 16, 1024], P('tile', 'col')
- gram: float32 [16, 16], replicated
Inputs may be any that keep to these rules, and one draw needn't show every extreme that they name: `ocean_mask`: in every column of devices (4 x 4 tile blocks), at least one device has only ocean tiles. `tile_owner`: among the ocean tiles of one device at most 1 share an owner; the ocean tiles of one column of devices are spread over its 16 owners so that the owners' counts differ by at most one. Land tiles carry an owner that is not used.
All inputs are finite; a program needn't handle non-finite values.
Results may differ from a plain program's by a relative error of at most 0.00014.
Values sent between devices are 32-bit elements; how exact they have to be, the bound alone decides.
No kernel may reach another device: no remote copies, remote signals or barrier semaphores. Data moves between devices by JAX's collectives and lax.ppermute only.
A program may use at most 192 MiB of HBM per device.

v0:
```python
import jax
import jax.numpy as jnp
from jax import lax
from jax.sharding import PartitionSpec as P

PASSES = 8
KAPPA = 0.2


def with_halo(cells, sides, width):
    for axis, dim in sides:
        count = lax.axis_size(axis)
        head = lax.slice_in_dim(cells, 0, width, axis=dim)
        tail = lax.slice_in_dim(cells, cells.shape[dim] - width, cells.shape[dim], axis=dim)
        cells = jnp.concatenate(
            [
                lax.ppermute(tail, axis, [(i, (i + 1) % count) for i in range(count)]),
                cells,
                lax.ppermute(head, axis, [((i + 1) % count, i) for i in range(count)]),
            ],
            axis=dim,
        )
    return cells


def quarter(first, second, turns):
    cosine = jnp.where(turns == 0, 1.0, jnp.where(turns == 2, -1.0, 0.0)).astype(first.dtype)
    sine = jnp.where(turns == 1, 1.0, jnp.where(turns == 3, -1.0, 0.0)).astype(first.dtype)
    return (cosine * first - sine * second, sine * first + cosine * second)


def turn_rims(padded, width, k_top, k_bottom):
    top_u, top_v = quarter(padded[0, :width], padded[1, :width], k_top)
    low_u, low_v = quarter(padded[0, -width:], padded[1, -width:], k_bottom)
    upper = jnp.stack([top_u, top_v])
    lower = jnp.stack([low_u, low_v])
    return jnp.concatenate([upper, padded[:, width:-width], lower], axis=1)


def relax(padded):
    centre = padded[:, 1:-1, 1:-1]
    beside_all = (
        padded[:, :-2, 1:-1] + padded[:, 2:, 1:-1] + padded[:, 1:-1, :-2] + padded[:, 1:-1, 2:]
    )
    return centre + KAPPA * (beside_all - 4.0 * centre)


def derive(padded):
    first = padded[..., 0, :, :]
    second = padded[..., 1, :, :]
    u_part = first[..., 1:-1, 1:-1]
    v_part = second[..., 1:-1, 1:-1]
    u_dx = (first[..., 1:-1, 2:] - first[..., 1:-1, :-2]) * 0.5
    u_dy = (first[..., 2:, 1:-1] - first[..., :-2, 1:-1]) * 0.5
    v_dx = (second[..., 1:-1, 2:] - second[..., 1:-1, :-2]) * 0.5
    v_dy = (second[..., 2:, 1:-1] - second[..., :-2, 1:-1]) * 0.5
    return jnp.stack([u_part, v_part, v_dx - u_dy, u_dy + v_dx, u_dx - v_dy], axis=-3)


def make_terms(base):
    u_part = base[..., 0, :]
    v_part = base[..., 1, :]
    vort = base[..., 2, :]
    strain = base[..., 3, :]
    stretch = base[..., 4, :]
    listed = [
        u_part,
        v_part,
        vort,
        strain,
        stretch,
        vort * vort,
        vort * strain,
        vort * stretch,
        strain * strain,
        stretch * stretch,
        strain * stretch,
        u_part * vort,
        v_part * vort,
        u_part * strain,
        v_part * stretch,
        u_part * v_part,
    ]
    return jnp.stack(listed, axis=-2)


def to_tiles(field, grid_x, grid_y, side):
    leading = field.shape[:-2]
    shaped = field.reshape(leading + (grid_x, side, grid_y, side))
    shaped = jnp.swapaxes(shaped, -3, -2)
    return shaped.reshape(leading + (grid_x * grid_y, side * side))


def per_device(u_velocity, v_velocity, ocean_mask, tile_owner, lower_edge_quarter_turns):
    rows_tile = lax.axis_size("tile")
    here = lax.axis_index("tile")
    k_top = lower_edge_quarter_turns[here]
    k_bottom = (4 - lower_edge_quarter_turns[(here + 1) % rows_tile]) % 4
    field = jnp.stack([u_velocity, v_velocity])
    for step in range(PASSES):
        padded = with_halo(field, (("tile", 1), ("col", 2)), 1)
        field = relax(turn_rims(padded, 1, k_top, k_bottom))
    fine_rows, fine_cols = u_velocity.shape
    coarse = field.reshape(2, fine_rows // 4, 4, fine_cols // 4, 4).mean(axis=(2, 4))
    coarse_pad = with_halo(coarse, (("tile", 1), ("col", 2)), 1)
    coarse_pad = turn_rims(coarse_pad, 1, k_top, k_bottom)
    grid_x, grid_y = ocean_mask.shape
    side = coarse.shape[1] // grid_x
    starting_tile_set = jnp.swapaxes(to_tiles(derive(coarse_pad), grid_x, grid_y, side), 0, 1)
    live = ocean_mask.reshape(-1) == 1
    owners = tile_owner.reshape(-1)
    tiles = live.shape[0]
    slots = tiles // rows_tile
    local = jnp.arange(tiles, dtype=jnp.int32)
    same = (owners[:, None] == owners[None, :]) & live[None, :] & (local[None, :] < local[:, None])
    slot = jnp.sum(same.astype(jnp.int32), axis=1)
    target = jnp.arange(rows_tile * slots, dtype=jnp.int32)
    chosen_terms = (
        live[None, :]
        & (owners[None, :] == target[:, None] // slots)
        & (slot[None, :] == target[:, None] % slots)
    ).astype(jnp.float32)
    library = make_terms(
        lax.all_to_all(
            jnp.einsum(
                "vh,hsd->vsd", chosen_terms, starting_tile_set, precision=lax.Precision.HIGHEST
            ),
            "tile",
            split_axis=0,
            concat_axis=0,
            tiled=True,
        )
    )
    part = jnp.einsum("pnc,pmc->nm", library, library, precision=lax.Precision.HIGHEST)
    gram = lax.psum(part, ("tile", "col")) / (fine_rows // 4 * (fine_cols // 4))
    return (library[None, None], gram)


def solution(mesh):
    in_specs = (P("tile", "col"), P("tile", "col"), P("tile", "col"), P("tile", "col"), P())
    out_specs = (P("tile", "col", None, None, None), P())
    return jax.shard_map(
        per_device, mesh=mesh, in_specs=in_specs, out_specs=out_specs, check_vma=False
    )
```

profile of v0, /device:TPU:1, one launch (start us, length us, event | category | flops | bytes accessed | tf_op | source)
XLA Modules:
  0.0 374.1 jit_solution(4603771623657914441)
XLA Ops:
  8.2 3.5 collective-permute-start.2
  21.4 6.4 %fusion.45 = f32[2,512,512]{2,1,0:T(8,128)S(1)} fusion(f32[2,514,1]{2,1,0:T(8,128)} %copy-done.15, f32[2,1,512]{2,1,0:T(1,128)S(1)} %collective-permute-done.1, f32[2,1,512]{2,1,0:T(1,128)S(1)} %collective-permute-done, f32[1,512,512]{2,1,0:T(8,128)S(1)} %bitcast.34, f32[1,512,512]{2,1,0:T(8,128)S(1)} %bitcast.28, f32[2,514,1]{2,1,0:T(8,128)} %copy-done.13, ...), kind=kLoop, calls=%fused_computation.129 | loop fusion | flops 10485760 | bytes 6324288 | tf_op jit(solution)/shard_map/add | solution.py:45
  34.3 4.6 %collective-permute-start.7 = (f32[2,514,1]{1,0,2:T(2,128)S(1)}, f32[2,514,1]{1,0,2:T(2,128)S(1)}, u32[]{:S(2)}, u32[]{:S(2)}) collective-permute-start(f32[2,514,1]{1,0,2:T(2,128)S(1)} %copy.209), channel_id=1, source_target_pairs={{1,0},{2,1},{3,2},{4,3},{5,4},{6,5},{7,6},{0,7},{9,8},{10,9},{11,1... | collective-permute-start | bytes 12344 | tf_op jit(solution)/shard_map/ppermute | solution.py:19
  44.0 8.1 %fusion.39 = f32[2,512,512]{2,1,0:T(8,128)S(1)} fusion(f32[2,512,512]{2,1,0:T(8,128)} %copy-done.9, f32[2,514,1]{2,1,0:T(8,128)S(1)} %copy-done.16, f32[2,1,512]{2,1,0:T(1,128)S(1)} %collective-permute-done.5, f32[2,1,512]{2,1,0:T(1,128)S(1)} %collective-permute-done.4, f32[2,514,1]{2,1,0:T(8,128)} %copy-done.14, f32[2,512,514]{2,1,0:T(8,128)S(1)} %slice.600, ...), kind=kLoop, calls=%fused_computation.113 | loop fusion | flops 8912896 | bytes 6324288 | tf_op jit(solution)/shard_map/add | solution.py:45
  59.6 3.8 %collective-permute-start.11 = (f32[2,514,1]{1,0,2:T(2,128)S(1)}, f32[2,514,1]{1,0,2:T(2,128)S(1)}, u32[]{:S(2)}, u32[]{:S(2)}) collective-permute-start(f32[2,514,1]{1,0,2:T(2,128)S(1)} %copy.215), channel_id=1, source_target_pairs={{1,0},{2,1},{3,2},{4,3},{5,4},{6,5},{7,6},{0,7},{9,8},{10,9},{11,1... | collective-permute-start | bytes 12344 | tf_op jit(solution)/shard_map/ppermute | solution.py:19
  66.1 5.0 %fusion.33 = f32[2,512,512]{2,1,0:T(8,128)S(1)} fusion(f32[2,512,512]{2,1,0:T(8,128)S(1)} %fusion.39, f32[2,514,1]{2,1,0:T(8,128)S(1)} %copy.217, f32[2,1,512]{2,1,0:T(1,128)S(1)} %collective-permute-done.9, f32[2,1,512]{2,1,0:T(1,128)S(1)} %collective-permute-done.8, f32[2,514,1]{2,1,0:T(8,128)S(1)} %copy.216, f32[2,512,514]{2,1,0:T(8,128)S(1)} %slice.603, ...), kind=kLoop, calls=%fused_computation.97 | loop fusion | flops 8912896 | bytes 6324288 | tf_op jit(solution)/shard_map/add | solution.py:45
  71.8 4.6 %collective-permute-start.13 = (f32[2,1,512]{2,1,0:T(1,128)S(1)}, f32[2,1,512]{2,1,0:T(1,128)S(1)}, u32[]{:S(2)}, u32[]{:S(2)}) collective-permute-start(f32[2,1,512]{2,1,0:T(1,128)S(1)} %get-tuple-element.85), channel_id=1, source_target_pairs={{8,0},{16,8},{24,16},{32,24},{40,32},{48,40},{56,48},{64,56},{72,6... | collective-permute-start | bytes 12296 | tf_op jit(solution)/shard_map/ppermute | solution.py:19
  79.9 3.6 collective-permute-start.15
  86.0 5.0 %fusion.27 = f32[2,512,512]{2,1,0:T(8,128)S(1)} fusion(f32[2,512,512]{2,1,0:T(8,128)S(1)} %copy-done.1, f32[2,514,1]{2,1,0:T(8,128)S(1)} %copy.223, f32[2,1,512]{2,1,0:T(1,128)S(1)} %collective-permute-done.13, f32[2,1,512]{2,1,0:T(1,128)S(1)} %collective-permute-done.12, f32[2,514,1]{2,1,0:T(8,128)S(1)} %copy.222, f32[2,512,514]{2,1,0:T(8,128)S(1)} %slice.606, ...), kind=kLoop, calls=%fused_computation.81 | loop fusion | flops 8912896 | bytes 6324288 | tf_op jit(solution)/shard_map/add | solution.py:45
  91.0 5.6 %collective-permute-start.17 = (f32[2,1,512]{2,1,0:T(1,128)S(1)}, f32[2,1,512]{2,1,0:T(1,128)S(1)}, u32[]{:S(2)}, u32[]{:S(2)}) collective-permute-start(f32[2,1,512]{2,1,0:T(1,128)S(1)} %get-tuple-element.83), channel_id=1, source_target_pairs={{8,0},{16,8},{24,16},{32,24},{40,32},{48,40},{56,48},{64,56},{72,6... | collective-permute-start | bytes 12296 | tf_op jit(solution)/shard_map/ppermute | solution.py:19
  106.4 5.0 %fusion.21 = f32[2,512,512]{2,1,0:T(8,128)S(1)} fusion(f32[2,512,512]{2,1,0:T(8,128)S(1)} %copy-done.3, f32[2,514,1]{2,1,0:T(8,128)S(1)} %copy.229, f32[2,1,512]{2,1,0:T(1,128)S(1)} %collective-permute-done.17, f32[2,1,512]{2,1,0:T(1,128)S(1)} %collective-permute-done.16, f32[2,514,1]{2,1,0:T(8,128)S(1)} %copy.228, f32[2,512,514]{2,1,0:T(8,128)S(1)} %slice.609, ...), kind=kLoop, calls=%fused_computation.65 | loop fusion | flops 8912896 | bytes 6324288 | tf_op jit(solution)/shard_map/add | solution.py:45
  111.5 5.8 %collective-permute-start.21 = (f32[2,1,512]{2,1,0:T(1,128)S(1)}, f32[2,1,512]{2,1,0:T(1,128)S(1)}, u32[]{:S(2)}, u32[]{:S(2)}) collective-permute-start(f32[2,1,512]{2,1,0:T(1,128)S(1)} %get-tuple-element.81), channel_id=1, source_target_pairs={{8,0},{16,8},{24,16},{32,24},{40,32},{48,40},{56,48},{64,56},{72,6... | collective-permute-start | bytes 12296 | tf_op jit(solution)/shard_map/ppermute | solution.py:19
  121.1 3.3 collective-permute-start.23
  127.2 5.0 %fusion.15 = f32[2,512,512]{2,1,0:T(8,128)S(1)} fusion(f32[2,512,512]{2,1,0:T(8,128)S(1)} %copy-done.5, f32[2,514,1]{2,1,0:T(8,128)S(1)} %copy.235, f32[2,1,512]{2,1,0:T(1,128)S(1)} %collective-permute-done.21, f32[2,1,512]{2,1,0:T(1,128)S(1)} %collective-permute-done.20, f32[2,514,1]{2,1,0:T(8,128)S(1)} %copy.234, f32[2,512,514]{2,1,0:T(8,128)S(1)} %slice.612, ...), kind=kLoop, calls=%fused_computation.49 | loop fusion | flops 8912896 | bytes 6324288 | tf_op jit(solution)/shard_map/add | solution.py:45
  132.3 5.8 %collective-permute-start.25 = (f32[2,1,512]{2,1,0:T(1,128)S(1)}, f32[2,1,512]{2,1,0:T(1,128)S(1)}, u32[]{:S(2)}, u32[]{:S(2)}) collective-permute-start(f32[2,1,512]{2,1,0:T(1,128)S(1)} %get-tuple-element.79), channel_id=1, source_target_pairs={{8,0},{16,8},{24,16},{32,24},{40,32},{48,40},{56,48},{64,56},{72,6... | collective-permute-start | bytes 12296 | tf_op jit(solution)/shard_map/ppermute | solution.py:19
  149.0 4.9 %fusion.9 = f32[2,512,512]{2,1,0:T(8,128)S(1)} fusion(f32[2,512,512]{2,1,0:T(8,128)S(1)} %copy-done.8, f32[2,514,1]{2,1,0:T(8,128)S(1)} %copy.241, f32[2,1,512]{2,1,0:T(1,128)S(1)} %collective-permute-done.25, f32[2,1,512]{2,1,0:T(1,128)S(1)} %collective-permute-done.24, f32[2,514,1]{2,1,0:T(8,128)S(1)} %copy.240, f32[2,512,514]{2,1,0:T(8,128)S(1)} %slice.615, ...), kind=kLoop, calls=%fused_computation.33 | loop fusion | flops 8912896 | bytes 6324288 | tf_op jit(solution)/shard_map/add | solution.py:45
  154.1 5.8 %collective-permute-start.29 = (f32[2,1,512]{2,1,0:T(1,128)S(1)}, f32[2,1,512]{2,1,0:T(1,128)S(1)}, u32[]{:S(2)}, u32[]{:S(2)}) collective-permute-start(f32[2,1,512]{2,1,0:T(1,128)S(1)} %get-tuple-element.77), channel_id=1, source_target_pairs={{8,0},{16,8},{24,16},{32,24},{40,32},{48,40},{56,48},{64,56},{72,6... | collective-permute-start | bytes 12296 | tf_op jit(solution)/shard_map/ppermute | solution.py:19
  169.6 5.9 %fusion.3 = f32[2,512,512]{2,1,0:T(8,128)} fusion(f32[2,512,512]{2,1,0:T(8,128)S(1)} %fusion.9, f32[2,514,1]{2,1,0:T(8,128)S(1)} %copy.247, f32[2,1,512]{2,1,0:T(1,128)S(1)} %collective-permute-done.29, f32[2,1,512]{2,1,0:T(1,128)S(1)} %collective-permute-done.28, f32[2,514,1]{2,1,0:T(8,128)S(1)} %copy.246, f32[2,512,514]{2,1,0:T(8,128)S(1)} %slice.618, ...), kind=kLoop, calls=%fused_computation.17 | loop fusion | flops 8912896 | bytes 6324288 | tf_op jit(solution)/shard_map/add | solution.py:45
  175.5 71.4 %reshape.326 = f32[2,128,4,128,4]{4,3,2,1,0:T(8,128)} reshape(f32[2,512,512]{2,1,0:T(8,128)} %fusion.3) | data formatting | bytes 4194304 | tf_op jit(solution)/shard_map/reshape | solution.py:104
  246.9 20.8 %reduce_sum.19 = f32[2,128,128]{2,1,0:T(8,128)S(1)} reduce(f32[2,128,4,128,4]{4,3,2,1,0:T(8,128)} %reshape.326, f32[]{:T(128)} %constant.89.clone.1), dimensions={2,4}, to_apply=%region_1.2 | reduce | flops 491520 | bytes 2228228 | tf_op jit(solution)/shard_map/reduce_sum | solution.py:104
  267.8 5.7 %collective-permute-start.33 = (f32[2,1,128]{2,1,0:T(1,128)S(1)}, f32[2,1,128]{2,1,0:T(1,128)S(1)}, u32[]{:S(2)}, u32[]{:S(2)}) collective-permute-start(f32[2,1,128]{2,1,0:T(1,128)S(1)} %get-tuple-element.113), channel_id=1, source_target_pairs={{8,0},{16,8},{24,16},{32,24},{40,32},{48,40},{56,48},{64,56},{72,6... | collective-permute-start | bytes 3080 | tf_op jit(solution)/shard_map/ppermute | solution.py:19
  274.4 4.0 %collective-permute-start.34 = (f32[2,130,1]{2,1,0:T(8,128)S(1)}, f32[2,130,1]{2,1,0:T(8,128)S(1)}, u32[]{:S(2)}, u32[]{:S(2)}) collective-permute-start(f32[2,130,1]{2,1,0:T(8,128)S(1)} %get-tuple-element.110), channel_id=1, source_target_pairs={{0,1},{1,2},{2,3},{3,4},{4,5},{5,6},{6,7},{7,0},{8,9},{9,10},{10,1... | collective-permute-start | bytes 3128 | tf_op jit(solution)/shard_map/ppermute | solution.py:17
  286.9 18.4 %all_to_all.5 = f32[16,5,1024]{2,1,0:T(8,128)S(1)} all-to-all(f32[16,5,1024]{2,1,0:T(8,128)S(1)} %copy.251), channel_id=1, replica_groups=mesh['tile'=16,'col'=8] {'tile'}, dimensions={0} | all-to-all | bytes 655360 | tf_op jit(solution)/shard_map/all_to_all | solution.py:124
  308.6 64.7 %psum.7 = f32[16,16]{1,0:T(8,128)S(1)} all-reduce(f32[16,16]{1,0:T(8,128)S(1)} %convolution_bitcast_fusion), channel_id=1, replica_groups=mesh['tile'=16,'col'=8] {'tile','col'}, use_global_device_ids=true, to_apply=%region_2.3 | all-reduce | flops 256 | bytes 2048 | tf_op jit(solution)/shard_map/psum | solution.py:135
  (234 shorter events, 92.4 us)
Async XLA Ops:
  8.2 10.1 %collective-permute-start.2 = (f32[2,514,1]{1,0,2:T(2,128)S(1)}, f32[2,514,1]{1,0,2:T(2,128)S(1)}, u32[]{:S(2)}, u32[]{:S(2)}) collective-permute-start(f32[2,514,1]{1,0,2:T(2,128)S(1)} %copy.202), channel_id=1, source_target_pairs={{0,1},{1,2},{2,3},{3,4},{4,5},{5,6},{6,7},{7,0},{8,9},{9,10},{10,1... | collective-permute-start | bytes 12344 | tf_op jit(solution)/shard_map/ppermute | solution.py:17
  12.0 6.6 %collective-permute-start.3 = (f32[2,514,1]{1,0,2:T(2,128)S(1)}, f32[2,514,1]{1,0,2:T(2,128)S(1)}, u32[]{:S(2)}, u32[]{:S(2)}) collective-permute-start(f32[2,514,1]{1,0,2:T(2,128)S(1)} %copy.203), channel_id=1, source_target_pairs={{1,0},{2,1},{3,2},{4,3},{5,4},{6,5},{7,6},{0,7},{9,8},{10,9},{11,1... | collective-permute-start | bytes 12344 | tf_op jit(solution)/shard_map/ppermute | solution.py:19
  33.3 6.1 %collective-permute-start.6 = (f32[2,514,1]{1,0,2:T(2,128)S(1)}, f32[2,514,1]{1,0,2:T(2,128)S(1)}, u32[]{:S(2)}, u32[]{:S(2)}) collective-permute-start(f32[2,514,1]{1,0,2:T(2,128)S(1)} %copy.208), channel_id=1, source_target_pairs={{0,1},{1,2},{2,3},{3,4},{4,5},{5,6},{6,7},{7,0},{8,9},{9,10},{10,1... | collective-permute-start | bytes 12344 | tf_op jit(solution)/shard_map/ppermute | solution.py:17
  34.3 5.4 %collective-permute-start.7 = (f32[2,514,1]{1,0,2:T(2,128)S(1)}, f32[2,514,1]{1,0,2:T(2,128)S(1)}, u32[]{:S(2)}, u32[]{:S(2)}) collective-permute-start(f32[2,514,1]{1,0,2:T(2,128)S(1)} %copy.209), channel_id=1, source_target_pairs={{1,0},{2,1},{3,2},{4,3},{5,4},{6,5},{7,6},{0,7},{9,8},{10,9},{11,1... | collective-permute-start | bytes 12344 | tf_op jit(solution)/shard_map/ppermute | solution.py:19
  57.6 6.6 %collective-permute-start.10 = (f32[2,514,1]{1,0,2:T(2,128)S(1)}, f32[2,514,1]{1,0,2:T(2,128)S(1)}, u32[]{:S(2)}, u32[]{:S(2)}) collective-permute-start(f32[2,514,1]{1,0,2:T(2,128)S(1)} %copy.214), channel_id=1, source_target_pairs={{0,1},{1,2},{2,3},{3,4},{4,5},{5,6},{6,7},{7,0},{8,9},{9,10},{10,1... | collective-permute-start | bytes 12344 | tf_op jit(solution)/shard_map/ppermute | solution.py:17
  71.1 5.9 %collective-permute-start.12 = (f32[2,1,512]{2,1,0:T(1,128)S(1)}, f32[2,1,512]{2,1,0:T(1,128)S(1)}, u32[]{:S(2)}, u32[]{:S(2)}) collective-permute-start(f32[2,1,512]{2,1,0:T(1,128)S(1)} %get-tuple-element.84), channel_id=1, source_target_pairs={{0,8},{8,16},{16,24},{24,32},{32,40},{40,48},{48,56},{56,64},{64,7... | collective-permute-start | bytes 12296 | tf_op jit(solution)/shard_map/ppermute | solution.py:17
  71.8 5.4 %collective-permute-start.13 = (f32[2,1,512]{2,1,0:T(1,128)S(1)}, f32[2,1,512]{2,1,0:T(1,128)S(1)}, u32[]{:S(2)}, u32[]{:S(2)}) collective-permute-start(f32[2,1,512]{2,1,0:T(1,128)S(1)} %get-tuple-element.85), channel_id=1, source_target_pairs={{8,0},{16,8},{24,16},{32,24},{40,32},{48,40},{56,48},{64,56},{72,6... | collective-permute-start | bytes 12296 | tf_op jit(solution)/shard_map/ppermute | solution.py:19
  77.7 6.4 %collective-permute-start.14 = (f32[2,514,1]{1,0,2:T(2,128)S(1)}, f32[2,514,1]{1,0,2:T(2,128)S(1)}, u32[]{:S(2)}, u32[]{:S(2)}) collective-permute-start(f32[2,514,1]{1,0,2:T(2,128)S(1)} %copy.220), channel_id=1, source_target_pairs={{0,1},{1,2},{2,3},{3,4},{4,5},{5,6},{6,7},{7,0},{8,9},{9,10},{10,1... | collective-permute-start | bytes 12344 | tf_op jit(solution)/shard_map/ppermute | solution.py:17
  90.9 6.3 %collective-permute-start.16 = (f32[2,1,512]{2,1,0:T(1,128)S(1)}, f32[2,1,512]{2,1,0:T(1,128)S(1)}, u32[]{:S(2)}, u32[]{:S(2)}) collective-permute-start(f32[2,1,512]{2,1,0:T(1,128)S(1)} %get-tuple-element.82), channel_id=1, source_target_pairs={{0,8},{8,16},{16,24},{24,32},{32,40},{40,48},{48,56},{56,64},{64,7... | collective-permute-start | bytes 12296 | tf_op jit(solution)/shard_map/ppermute | solution.py:17
  91.0 6.4 %collective-permute-start.17 = (f32[2,1,512]{2,1,0:T(1,128)S(1)}, f32[2,1,512]{2,1,0:T(1,128)S(1)}, u32[]{:S(2)}, u32[]{:S(2)}) collective-permute-start(f32[2,1,512]{2,1,0:T(1,128)S(1)} %get-tuple-element.83), channel_id=1, source_target_pairs={{8,0},{16,8},{24,16},{32,24},{40,32},{48,40},{56,48},{64,56},{72,6... | collective-permute-start | bytes 12296 | tf_op jit(solution)/shard_map/ppermute | solution.py:19
  97.9 6.3 %collective-permute-start.18 = (f32[2,514,1]{1,0,2:T(2,128)S(1)}, f32[2,514,1]{1,0,2:T(2,128)S(1)}, u32[]{:S(2)}, u32[]{:S(2)}) collective-permute-start(f32[2,514,1]{1,0,2:T(2,128)S(1)} %copy.226), channel_id=1, source_target_pairs={{0,1},{1,2},{2,3},{3,4},{4,5},{5,6},{6,7},{7,0},{8,9},{9,10},{10,1... | collective-permute-start | bytes 12344 | tf_op jit(solution)/shard_map/ppermute | solution.py:17
  111.4 6.4 %collective-permute-start.20 = (f32[2,1,512]{2,1,0:T(1,128)S(1)}, f32[2,1,512]{2,1,0:T(1,128)S(1)}, u32[]{:S(2)}, u32[]{:S(2)}) collective-permute-start(f32[2,1,512]{2,1,0:T(1,128)S(1)} %get-tuple-element.80), channel_id=1, source_target_pairs={{0,8},{8,16},{16,24},{24,32},{32,40},{40,48},{48,56},{56,64},{64,7... | collective-permute-start | bytes 12296 | tf_op jit(solution)/shard_map/ppermute | solution.py:17
  111.5 6.6 %collective-permute-start.21 = (f32[2,1,512]{2,1,0:T(1,128)S(1)}, f32[2,1,512]{2,1,0:T(1,128)S(1)}, u32[]{:S(2)}, u32[]{:S(2)}) collective-permute-start(f32[2,1,512]{2,1,0:T(1,128)S(1)} %get-tuple-element.81), channel_id=1, source_target_pairs={{8,0},{16,8},{24,16},{32,24},{40,32},{48,40},{56,48},{64,56},{72,6... | collective-permute-start | bytes 12296 | tf_op jit(solution)/shard_map/ppermute | solution.py:19
  118.6 6.1 %collective-permute-start.22 = (f32[2,514,1]{1,0,2:T(2,128)S(1)}, f32[2,514,1]{1,0,2:T(2,128)S(1)}, u32[]{:S(2)}, u32[]{:S(2)}) collective-permute-start(f32[2,514,1]{1,0,2:T(2,128)S(1)} %copy.232), channel_id=1, source_target_pairs={{0,1},{1,2},{2,3},{3,4},{4,5},{5,6},{6,7},{7,0},{8,9},{9,10},{10,1... | collective-permute-start | bytes 12344 | tf_op jit(solution)/shard_map/ppermute | solution.py:17
  132.2 6.4 %collective-permute-start.24 = (f32[2,1,512]{2,1,0:T(1,128)S(1)}, f32[2,1,512]{2,1,0:T(1,128)S(1)}, u32[]{:S(2)}, u32[]{:S(2)}) collective-permute-start(f32[2,1,512]{2,1,0:T(1,128)S(1)} %get-tuple-element.78), channel_id=1, source_target_pairs={{0,8},{8,16},{16,24},{24,32},{32,40},{40,48},{48,56},{56,64},{64,7... | collective-permute-start | bytes 12296 | tf_op jit(solution)/shard_map/ppermute | solution.py:17
  132.3 6.6 %collective-permute-start.25 = (f32[2,1,512]{2,1,0:T(1,128)S(1)}, f32[2,1,512]{2,1,0:T(1,128)S(1)}, u32[]{:S(2)}, u32[]{:S(2)}) collective-permute-start(f32[2,1,512]{2,1,0:T(1,128)S(1)} %get-tuple-element.79), channel_id=1, source_target_pairs={{8,0},{16,8},{24,16},{32,24},{40,32},{48,40},{56,48},{64,56},{72,6... | collective-permute-start | bytes 12296 | tf_op jit(solution)/shard_map/ppermute | solution.py:19
  139.3 6.1 %collective-permute-start.26 = (f32[2,514,1]{1,0,2:T(2,128)S(1)}, f32[2,514,1]{1,0,2:T(2,128)S(1)}, u32[]{:S(2)}, u32[]{:S(2)}) collective-permute-start(f32[2,514,1]{1,0,2:T(2,128)S(1)} %copy.238), channel_id=1, source_target_pairs={{0,1},{1,2},{2,3},{3,4},{4,5},{5,6},{6,7},{7,0},{8,9},{9,10},{10,1... | collective-permute-start | bytes 12344 | tf_op jit(solution)/shard_map/ppermute | solution.py:17
  154.0 6.4 %collective-permute-start.28 = (f32[2,1,512]{2,1,0:T(1,128)S(1)}, f32[2,1,512]{2,1,0:T(1,128)S(1)}, u32[]{:S(2)}, u32[]{:S(2)}) collective-permute-start(f32[2,1,512]{2,1,0:T(1,128)S(1)} %get-tuple-element.76), channel_id=1, source_target_pairs={{0,8},{8,16},{16,24},{24,32},{32,40},{40,48},{48,56},{56,64},{64,7... | collective-permute-start | bytes 12296 | tf_op jit(solution)/shard_map/ppermute | solution.py:17
  154.1 6.6 %collective-permute-start.29 = (f32[2,1,512]{2,1,0:T(1,128)S(1)}, f32[2,1,512]{2,1,0:T(1,128)S(1)}, u32[]{:S(2)}, u32[]{:S(2)}) collective-permute-start(f32[2,1,512]{2,1,0:T(1,128)S(1)} %get-tuple-element.77), channel_id=1, source_target_pairs={{8,0},{16,8},{24,16},{32,24},{40,32},{48,40},{56,48},{64,56},{72,6... | collective-permute-start | bytes 12296 | tf_op jit(solution)/shard_map/ppermute | solution.py:19
  161.1 6.1 %collective-permute-start.30 = (f32[2,514,1]{1,0,2:T(2,128)S(1)}, f32[2,514,1]{1,0,2:T(2,128)S(1)}, u32[]{:S(2)}, u32[]{:S(2)}) collective-permute-start(f32[2,514,1]{1,0,2:T(2,128)S(1)} %copy.244), channel_id=1, source_target_pairs={{0,1},{1,2},{2,3},{3,4},{4,5},{5,6},{6,7},{7,0},{8,9},{9,10},{10,1... | collective-permute-start | bytes 12344 | tf_op jit(solution)/shard_map/ppermute | solution.py:17
  267.7 6.3 %collective-permute-start.32 = (f32[2,1,128]{2,1,0:T(1,128)S(1)}, f32[2,1,128]{2,1,0:T(1,128)S(1)}, u32[]{:S(2)}, u32[]{:S(2)}) collective-permute-start(f32[2,1,128]{2,1,0:T(1,128)S(1)} %get-tuple-element.112), channel_id=1, source_target_pairs={{0,8},{8,16},{16,24},{24,32},{32,40},{40,48},{48,56},{56,64},{64,7... | collective-permute-start | bytes 3080 | tf_op jit(solution)/shard_map/ppermute | solution.py:17
  267.8 6.5 %collective-permute-start.33 = (f32[2,1,128]{2,1,0:T(1,128)S(1)}, f32[2,1,128]{2,1,0:T(1,128)S(1)}, u32[]{:S(2)}, u32[]{:S(2)}) collective-permute-start(f32[2,1,128]{2,1,0:T(1,128)S(1)} %get-tuple-element.113), channel_id=1, source_target_pairs={{8,0},{16,8},{24,16},{32,24},{40,32},{48,40},{56,48},{64,56},{72,6... | collective-permute-start | bytes 3080 | tf_op jit(solution)/shard_map/ppermute | solution.py:19
  274.4 7.6 %collective-permute-start.34 = (f32[2,130,1]{2,1,0:T(8,128)S(1)}, f32[2,130,1]{2,1,0:T(8,128)S(1)}, u32[]{:S(2)}, u32[]{:S(2)}) collective-permute-start(f32[2,130,1]{2,1,0:T(8,128)S(1)} %get-tuple-element.110), channel_id=1, source_target_pairs={{0,1},{1,2},{2,3},{3,4},{4,5},{5,6},{6,7},{7,0},{8,9},{9,10},{10,1... | collective-permute-start | bytes 3128 | tf_op jit(solution)/shard_map/ppermute | solution.py:17
  278.5 5.4 %collective-permute-start.35 = (f32[2,130,1]{2,1,0:T(8,128)S(1)}, f32[2,130,1]{2,1,0:T(8,128)S(1)}, u32[]{:S(2)}, u32[]{:S(2)}) collective-permute-start(f32[2,130,1]{2,1,0:T(8,128)S(1)} %get-tuple-element.111), channel_id=1, source_target_pairs={{1,0},{2,1},{3,2},{4,3},{5,4},{6,5},{7,6},{0,7},{9,8},{10,9},{11,1... | collective-permute-start | bytes 3128 | tf_op jit(solution)/shard_map/ppermute | solution.py:19
  (33 other events, 244.8 us)
where the time goes:
time: 381 us; the launch traced here: 374 us
  starting transfers between devices  91.9 us (24%)
  local copies, waits for them, and re-layouts  89.5 us (23%)
  blocking collectives  83.1 us (22%)
  other arithmetic  81.8 us (21%)
  waiting for transfers between devices  20.8 us (5%)
  between operations  5.18 us (1%)
    reshape x1, local copies, waits for them, and re-layouts, per_device(): field.reshape(2, fine_rows // 4, 4, fine_cols // 4, 4).mean(axis=(2, 4))  71.4 us
    psum x1, blocking collectives, per_device(): gram = lax.psum(part, ('tile', 'col')) / (fine_rows // 4 * (fine_cols // 4))  64.7 us
    ppermute x18, starting transfers between devices, with_halo(): lax.ppermute(head, axis, [((i + 1) % count, i) for i in range(count)])  64.6 us
    add x8, other arithmetic, relax(): return centre + KAPPA * (beside_all - 4.0 * centre)  45.1 us
    ppermute x18, starting transfers between devices, with_halo(): lax.ppermute(tail, axis, [(i, (i + 1) % count) for i in range(count)])  27.3 us
    reduce_sum x1, other arithmetic, per_device(): field.reshape(2, fine_rows // 4, 4, fine_cols // 4, 4).mean(axis=(2, 4))  20.8 us
    all_to_all x1, blocking collectives, per_device(): lax.all_to_all(jnp.einsum('vh,hsd->vsd', chosen_terms, starting_tile_set,...  18.4 us
    ppermute x18, waiting for transfers between devices, with_halo(): lax.ppermute(tail, axis, [(i, (i + 1) % count) for i in range(count)])  11.6 us
  transfers between devices with their start and end apart: 36, of which 31 were waited for; matrix products, arithmetic and copies ran while one was open for 1% of the time, Pallas kernels for 0%

commit v1 on v0

--- a/solution.py
+++ b/solution.py
@@ -132,7 +132,7 @@
         )
     )
     part = jnp.einsum("pnc,pmc->nm", library, library, precision=lax.Precision.HIGHEST)
-    gram = lax.psum(part, ("tile", "col")) / (fine_rows // 4 * (fine_cols // 4))
+    gram = lax.psum(lax.psum(part, "tile"), "col") / (fine_rows // 4 * (fine_cols // 4))
     return (library[None, None], gram)
 
 

time: 381 us -> 367 us (0.963)
  the two profiles are of different devices: /device:TPU:1 before, /device:TPU:0 now
where the time goes in v1:
time: 367 us; the launch traced here: 361 us
  local copies, waits for them, and re-layouts  89.5 us (24%)
  starting transfers between devices  88.6 us (24%)
  other arithmetic  81.8 us (22%)
  blocking collectives  65.4 us (18%)
  waiting for transfers between devices  28.3 us (8%)
  between operations  5.23 us (1%)
    reshape x1, local copies, waits for them, and re-layouts, per_device(): field.reshape(2, fine_rows // 4, 4, fine_cols // 4, 4).mean(axis=(2, 4))  71.4 us
    ppermute x18, starting transfers between devices, with_halo(): lax.ppermute(head, axis, [((i + 1) % count, i) for i in range(count)])  63.5 us
    add x8, other arithmetic, relax(): return centre + KAPPA * (beside_all - 4.0 * centre)  45.1 us
    psum x1, blocking collectives, per_device(): lax.psum(part, 'tile')  27.7 us
    ppermute x18, starting transfers between devices, with_halo(): lax.ppermute(tail, axis, [(i, (i + 1) % count) for i in range(count)])  25.1 us
    psum x1, blocking collectives, per_device(): lax.psum(lax.psum(part, 'tile'), 'col')  23.7 us
    ppermute x18, waiting for transfers between devices, with_halo(): lax.ppermute(tail, axis, [(i, (i + 1) % count) for i in range(count)])  22.7 us
    reduce_sum x1, other arithmetic, per_device(): field.reshape(2, fine_rows // 4, 4, fine_cols // 4, 4).mean(axis=(2, 4))  20.8 us
  transfers between devices with their start and end apart: 36, of which 23 were waited for; matrix products, arithmetic and copies ran while one was open for 1% of the time, Pallas kernels for 0%

profile of v1, /device:TPU:0, one launch (start us, length us, event | category | flops | bytes accessed | tf_op | source)
XLA Modules:
  0.0 360.6 jit_solution(15315674764877570627)
XLA Ops:
  7.3 4.0 %collective-permute-start.2 = (f32[2,514,1]{1,0,2:T(2,128)S(1)}, f32[2,514,1]{1,0,2:T(2,128)S(1)}, u32[]{:S(2)}, u32[]{:S(2)}) collective-permute-start(f32[2,514,1]{1,0,2:T(2,128)S(1)} %copy.202), channel_id=1, source_target_pairs={{0,1},{1,2},{2,3},{3,4},{4,5},{5,6},{6,7},{7,0},{8,9},{9,10},{10,1... | collective-permute-start | bytes 12344 | tf_op jit(solution)/shard_map/ppermute | solution.py:17
  20.9 6.4 %fusion.45 = f32[2,512,512]{2,1,0:T(8,128)S(1)} fusion(f32[2,514,1]{2,1,0:T(8,128)} %copy-done.15, f32[2,1,512]{2,1,0:T(1,128)S(1)} %collective-permute-done.1, f32[2,1,512]{2,1,0:T(1,128)S(1)} %collective-permute-done, f32[1,512,512]{2,1,0:T(8,128)S(1)} %bitcast.34, f32[1,512,512]{2,1,0:T(8,128)S(1)} %bitcast.28, f32[2,514,1]{2,1,0:T(8,128)} %copy-done.13, ...), kind=kLoop, calls=%fused_computation.129 | loop fusion | flops 10485760 | bytes 6324288 | tf_op jit(solution)/shard_map/add | solution.py:45
  27.4 3.8 %collective-permute-start.5 = (f32[2,1,512]{2,1,0:T(1,128)S(1)}, f32[2,1,512]{2,1,0:T(1,128)S(1)}, u32[]{:S(2)}, u32[]{:S(2)}) collective-permute-start(f32[2,1,512]{2,1,0:T(1,128)S(1)} %get-tuple-element.89), channel_id=1, source_target_pairs={{8,0},{16,8},{24,16},{32,24},{40,32},{48,40},{56,48},{64,56},{72,6... | collective-permute-start | bytes 12296 | tf_op jit(solution)/shard_map/ppermute | solution.py:19
  36.2 4.8 %collective-permute-start.7 = (f32[2,514,1]{1,0,2:T(2,128)S(1)}, f32[2,514,1]{1,0,2:T(2,128)S(1)}, u32[]{:S(2)}, u32[]{:S(2)}) collective-permute-start(f32[2,514,1]{1,0,2:T(2,128)S(1)} %copy.209), channel_id=1, source_target_pairs={{1,0},{2,1},{3,2},{4,3},{5,4},{6,5},{7,6},{0,7},{9,8},{10,9},{11,1... | collective-permute-start | bytes 12344 | tf_op jit(solution)/shard_map/ppermute | solution.py:19
  46.7 8.1 %fusion.39 = f32[2,512,512]{2,1,0:T(8,128)S(1)} fusion(f32[2,512,512]{2,1,0:T(8,128)} %copy-done.9, f32[2,514,1]{2,1,0:T(8,128)S(1)} %copy-done.16, f32[2,1,512]{2,1,0:T(1,128)S(1)} %collective-permute-done.5, f32[2,1,512]{2,1,0:T(1,128)S(1)} %collective-permute-done.4, f32[2,514,1]{2,1,0:T(8,128)} %copy-done.14, f32[2,512,514]{2,1,0:T(8,128)S(1)} %slice.600, ...), kind=kLoop, calls=%fused_computation.113 | loop fusion | flops 8912896 | bytes 6324288 | tf_op jit(solution)/shard_map/add | solution.py:45
  54.9 3.8 %collective-permute-start.9 = (f32[2,1,512]{2,1,0:T(1,128)S(1)}, f32[2,1,512]{2,1,0:T(1,128)S(1)}, u32[]{:S(2)}, u32[]{:S(2)}) collective-permute-start(f32[2,1,512]{2,1,0:T(1,128)S(1)} %get-tuple-element.87), channel_id=1, source_target_pairs={{8,0},{16,8},{24,16},{32,24},{40,32},{48,40},{56,48},{64,56},{72,6... | collective-permute-start | bytes 12296 | tf_op jit(solution)/shard_map/ppermute | solution.py:19
  62.8 3.8 %collective-permute-start.11 = (f32[2,514,1]{1,0,2:T(2,128)S(1)}, f32[2,514,1]{1,0,2:T(2,128)S(1)}, u32[]{:S(2)}, u32[]{:S(2)}) collective-permute-start(f32[2,514,1]{1,0,2:T(2,128)S(1)} %copy.215), channel_id=1, source_target_pairs={{1,0},{2,1},{3,2},{4,3},{5,4},{6,5},{7,6},{0,7},{9,8},{10,9},{11,1... | collective-permute-start | bytes 12344 | tf_op jit(solution)/shard_map/ppermute | solution.py:19
  69.9 5.0 %fusion.33 = f32[2,512,512]{2,1,0:T(8,128)S(1)} fusion(f32[2,512,512]{2,1,0:T(8,128)S(1)} %fusion.39, f32[2,514,1]{2,1,0:T(8,128)S(1)} %copy.217, f32[2,1,512]{2,1,0:T(1,128)S(1)} %collective-permute-done.9, f32[2,1,512]{2,1,0:T(1,128)S(1)} %collective-permute-done.8, f32[2,514,1]{2,1,0:T(8,128)S(1)} %copy.216, f32[2,512,514]{2,1,0:T(8,128)S(1)} %slice.603, ...), kind=kLoop, calls=%fused_computation.97 | loop fusion | flops 8912896 | bytes 6324288 | tf_op jit(solution)/shard_map/add | solution.py:45
  74.9 3.8 %collective-permute-start.13 = (f32[2,1,512]{2,1,0:T(1,128)S(1)}, f32[2,1,512]{2,1,0:T(1,128)S(1)}, u32[]{:S(2)}, u32[]{:S(2)}) collective-permute-start(f32[2,1,512]{2,1,0:T(1,128)S(1)} %get-tuple-element.85), channel_id=1, source_target_pairs={{8,0},{16,8},{24,16},{32,24},{40,32},{48,40},{56,48},{64,56},{72,6... | collective-permute-start | bytes 12296 | tf_op jit(solution)/shard_map/ppermute | solution.py:19
  90.1 5.0 %fusion.27 = f32[2,512,512]{2,1,0:T(8,128)S(1)} fusion(f32[2,512,512]{2,1,0:T(8,128)S(1)} %copy-done.1, f32[2,514,1]{2,1,0:T(8,128)S(1)} %copy.223, f32[2,1,512]{2,1,0:T(1,128)S(1)} %collective-permute-done.13, f32[2,1,512]{2,1,0:T(1,128)S(1)} %collective-permute-done.12, f32[2,514,1]{2,1,0:T(8,128)S(1)} %copy.222, f32[2,512,514]{2,1,0:T(8,128)S(1)} %slice.606, ...), kind=kLoop, calls=%fused_computation.81 | loop fusion | flops 8912896 | bytes 6324288 | tf_op jit(solution)/shard_map/add | solution.py:45
  95.1 3.8 %collective-permute-start.17 = (f32[2,1,512]{2,1,0:T(1,128)S(1)}, f32[2,1,512]{2,1,0:T(1,128)S(1)}, u32[]{:S(2)}, u32[]{:S(2)}) collective-permute-start(f32[2,1,512]{2,1,0:T(1,128)S(1)} %get-tuple-element.83), channel_id=1, source_target_pairs={{8,0},{16,8},{24,16},{32,24},{40,32},{48,40},{56,48},{64,56},{72,6... | collective-permute-start | bytes 12296 | tf_op jit(solution)/shard_map/ppermute | solution.py:19
  110.7 5.0 %fusion.21 = f32[2,512,512]{2,1,0:T(8,128)S(1)} fusion(f32[2,512,512]{2,1,0:T(8,128)S(1)} %copy-done.3, f32[2,514,1]{2,1,0:T(8,128)S(1)} %copy.229, f32[2,1,512]{2,1,0:T(1,128)S(1)} %collective-permute-done.17, f32[2,1,512]{2,1,0:T(1,128)S(1)} %collective-permute-done.16, f32[2,514,1]{2,1,0:T(8,128)S(1)} %copy.228, f32[2,512,514]{2,1,0:T(8,128)S(1)} %slice.609, ...), kind=kLoop, calls=%fused_computation.65 | loop fusion | flops 8912896 | bytes 6324288 | tf_op jit(solution)/shard_map/add | solution.py:45
  115.8 3.8 %collective-permute-start.21 = (f32[2,1,512]{2,1,0:T(1,128)S(1)}, f32[2,1,512]{2,1,0:T(1,128)S(1)}, u32[]{:S(2)}, u32[]{:S(2)}) collective-permute-start(f32[2,1,512]{2,1,0:T(1,128)S(1)} %get-tuple-element.81), channel_id=1, source_target_pairs={{8,0},{16,8},{24,16},{32,24},{40,32},{48,40},{56,48},{64,56},{72,6... | collective-permute-start | bytes 12296 | tf_op jit(solution)/shard_map/ppermute | solution.py:19
  131.4 5.0 %fusion.15 = f32[2,512,512]{2,1,0:T(8,128)S(1)} fusion(f32[2,512,512]{2,1,0:T(8,128)S(1)} %copy-done.5, f32[2,514,1]{2,1,0:T(8,128)S(1)} %copy.235, f32[2,1,512]{2,1,0:T(1,128)S(1)} %collective-permute-done.21, f32[2,1,512]{2,1,0:T(1,128)S(1)} %collective-permute-done.20, f32[2,514,1]{2,1,0:T(8,128)S(1)} %copy.234, f32[2,512,514]{2,1,0:T(8,128)S(1)} %slice.612, ...), kind=kLoop, calls=%fused_computation.49 | loop fusion | flops 8912896 | bytes 6324288 | tf_op jit(solution)/shard_map/add | solution.py:45
  136.5 3.8 %collective-permute-start.25 = (f32[2,1,512]{2,1,0:T(1,128)S(1)}, f32[2,1,512]{2,1,0:T(1,128)S(1)}, u32[]{:S(2)}, u32[]{:S(2)}) collective-permute-start(f32[2,1,512]{2,1,0:T(1,128)S(1)} %get-tuple-element.79), channel_id=1, source_target_pairs={{8,0},{16,8},{24,16},{32,24},{40,32},{48,40},{56,48},{64,56},{72,6... | collective-permute-start | bytes 12296 | tf_op jit(solution)/shard_map/ppermute | solution.py:19
  153.2 4.9 %fusion.9 = f32[2,512,512]{2,1,0:T(8,128)S(1)} fusion(f32[2,512,512]{2,1,0:T(8,128)S(1)} %copy-done.8, f32[2,514,1]{2,1,0:T(8,128)S(1)} %copy.241, f32[2,1,512]{2,1,0:T(1,128)S(1)} %collective-permute-done.25, f32[2,1,512]{2,1,0:T(1,128)S(1)} %collective-permute-done.24, f32[2,514,1]{2,1,0:T(8,128)S(1)} %copy.240, f32[2,512,514]{2,1,0:T(8,128)S(1)} %slice.615, ...), kind=kLoop, calls=%fused_computation.33 | loop fusion | flops 8912896 | bytes 6324288 | tf_op jit(solution)/shard_map/add | solution.py:45
  173.7 5.9 %fusion.3 = f32[2,512,512]{2,1,0:T(8,128)} fusion(f32[2,512,512]{2,1,0:T(8,128)S(1)} %fusion.9, f32[2,514,1]{2,1,0:T(8,128)S(1)} %copy.247, f32[2,1,512]{2,1,0:T(1,128)S(1)} %collective-permute-done.29, f32[2,1,512]{2,1,0:T(1,128)S(1)} %collective-permute-done.28, f32[2,514,1]{2,1,0:T(8,128)S(1)} %copy.246, f32[2,512,514]{2,1,0:T(8,128)S(1)} %slice.618, ...), kind=kLoop, calls=%fused_computation.17 | loop fusion | flops 8912896 | bytes 6324288 | tf_op jit(solution)/shard_map/add | solution.py:45
  179.6 71.4 %reshape.326 = f32[2,128,4,128,4]{4,3,2,1,0:T(8,128)} reshape(f32[2,512,512]{2,1,0:T(8,128)} %fusion.3) | data formatting | bytes 4194304 | tf_op jit(solution)/shard_map/reshape | solution.py:104
  251.0 20.8 %reduce_sum.19 = f32[2,128,128]{2,1,0:T(8,128)S(1)} reduce(f32[2,128,4,128,4]{4,3,2,1,0:T(8,128)} %reshape.326, f32[]{:T(128)} %constant.89.clone.1), dimensions={2,4}, to_apply=%region_1.2 | reduce | flops 491520 | bytes 2228228 | tf_op jit(solution)/shard_map/reduce_sum | solution.py:104
  271.9 3.8 %collective-permute-start.33 = (f32[2,1,128]{2,1,0:T(1,128)S(1)}, f32[2,1,128]{2,1,0:T(1,128)S(1)}, u32[]{:S(2)}, u32[]{:S(2)}) collective-permute-start(f32[2,1,128]{2,1,0:T(1,128)S(1)} %get-tuple-element.113), channel_id=1, source_target_pairs={{8,0},{16,8},{24,16},{32,24},{40,32},{48,40},{56,48},{64,56},{72,6... | collective-permute-start | bytes 3080 | tf_op jit(solution)/shard_map/ppermute | solution.py:19
  277.2 4.3 %collective-permute-start.34 = (f32[2,130,1]{2,1,0:T(8,128)S(1)}, f32[2,130,1]{2,1,0:T(8,128)S(1)}, u32[]{:S(2)}, u32[]{:S(2)}) collective-permute-start(f32[2,130,1]{2,1,0:T(8,128)S(1)} %get-tuple-element.110), channel_id=1, source_target_pairs={{0,1},{1,2},{2,3},{3,4},{4,5},{5,6},{6,7},{7,0},{8,9},{9,10},{10,1... | collective-permute-start | bytes 3128 | tf_op jit(solution)/shard_map/ppermute | solution.py:17
  291.1 14.1 %all_to_all.5 = f32[16,5,1024]{2,1,0:T(8,128)S(1)} all-to-all(f32[16,5,1024]{2,1,0:T(8,128)S(1)} %copy.251), channel_id=1, replica_groups=mesh['tile'=16,'col'=8] {'tile'}, dimensions={0} | all-to-all | bytes 655360 | tf_op jit(solution)/shard_map/all_to_all | solution.py:124
  308.4 27.7 %psum.14 = f32[16,16]{1,0:T(8,128)S(1)} all-reduce(f32[16,16]{1,0:T(8,128)S(1)} %convolution_bitcast_fusion), channel_id=1, replica_groups=mesh['tile'=16,'col'=8] {'tile'}, use_global_device_ids=true, to_apply=%region_2.3 | all-reduce | flops 256 | bytes 2048 | tf_op jit(solution)/shard_map/psum | solution.py:135
  336.1 23.7 %psum.15 = f32[16,16]{1,0:T(8,128)S(1)} all-reduce(f32[16,16]{1,0:T(8,128)S(1)} %psum.14), channel_id=1, replica_groups=mesh['tile'=16,'col'=8] {'col'}, use_global_device_ids=true, to_apply=%region_3.4 | all-reduce | flops 256 | bytes 2048 | tf_op jit(solution)/shard_map/psum | solution.py:135
  (235 shorter events, 108.8 us)
Async XLA Ops:
  7.3 10.6 %collective-permute-start.2 = (f32[2,514,1]{1,0,2:T(2,128)S(1)}, f32[2,514,1]{1,0,2:T(2,128)S(1)}, u32[]{:S(2)}, u32[]{:S(2)}) collective-permute-start(f32[2,514,1]{1,0,2:T(2,128)S(1)} %copy.202), channel_id=1, source_target_pairs={{0,1},{1,2},{2,3},{3,4},{4,5},{5,6},{6,7},{7,0},{8,9},{9,10},{10,1... | collective-permute-start | bytes 12344 | tf_op jit(solution)/shard_map/ppermute | solution.py:17
  11.5 6.6 %collective-permute-start.3 = (f32[2,514,1]{1,0,2:T(2,128)S(1)}, f32[2,514,1]{1,0,2:T(2,128)S(1)}, u32[]{:S(2)}, u32[]{:S(2)}) collective-permute-start(f32[2,514,1]{1,0,2:T(2,128)S(1)} %copy.203), channel_id=1, source_target_pairs={{1,0},{2,1},{3,2},{4,3},{5,4},{6,5},{7,6},{0,7},{9,8},{10,9},{11,1... | collective-permute-start | bytes 12344 | tf_op jit(solution)/shard_map/ppermute | solution.py:19
  27.3 5.2 %collective-permute-start.4 = (f32[2,1,512]{2,1,0:T(1,128)S(1)}, f32[2,1,512]{2,1,0:T(1,128)S(1)}, u32[]{:S(2)}, u32[]{:S(2)}) collective-permute-start(f32[2,1,512]{2,1,0:T(1,128)S(1)} %get-tuple-element.88), channel_id=1, source_target_pairs={{0,8},{8,16},{16,24},{24,32},{32,40},{40,48},{48,56},{56,64},{64,7... | collective-permute-start | bytes 12296 | tf_op jit(solution)/shard_map/ppermute | solution.py:17
  34.8 7.3 %collective-permute-start.6 = (f32[2,514,1]{1,0,2:T(2,128)S(1)}, f32[2,514,1]{1,0,2:T(2,128)S(1)}, u32[]{:S(2)}, u32[]{:S(2)}) collective-permute-start(f32[2,514,1]{1,0,2:T(2,128)S(1)} %copy.208), channel_id=1, source_target_pairs={{0,1},{1,2},{2,3},{3,4},{4,5},{5,6},{6,7},{7,0},{8,9},{9,10},{10,1... | collective-permute-start | bytes 12344 | tf_op jit(solution)/shard_map/ppermute | solution.py:17
  36.2 6.2 %collective-permute-start.7 = (f32[2,514,1]{1,0,2:T(2,128)S(1)}, f32[2,514,1]{1,0,2:T(2,128)S(1)}, u32[]{:S(2)}, u32[]{:S(2)}) collective-permute-start(f32[2,514,1]{1,0,2:T(2,128)S(1)} %copy.209), channel_id=1, source_target_pairs={{1,0},{2,1},{3,2},{4,3},{5,4},{6,5},{7,6},{0,7},{9,8},{10,9},{11,1... | collective-permute-start | bytes 12344 | tf_op jit(solution)/shard_map/ppermute | solution.py:19
  54.8 5.2 %collective-permute-start.8 = (f32[2,1,512]{2,1,0:T(1,128)S(1)}, f32[2,1,512]{2,1,0:T(1,128)S(1)}, u32[]{:S(2)}, u32[]{:S(2)}) collective-permute-start(f32[2,1,512]{2,1,0:T(1,128)S(1)} %get-tuple-element.86), channel_id=1, source_target_pairs={{0,8},{8,16},{16,24},{24,32},{32,40},{40,48},{48,56},{56,64},{64,7... | collective-permute-start | bytes 12296 | tf_op jit(solution)/shard_map/ppermute | solution.py:17
  60.5 7.5 %collective-permute-start.10 = (f32[2,514,1]{1,0,2:T(2,128)S(1)}, f32[2,514,1]{1,0,2:T(2,128)S(1)}, u32[]{:S(2)}, u32[]{:S(2)}) collective-permute-start(f32[2,514,1]{1,0,2:T(2,128)S(1)} %copy.214), channel_id=1, source_target_pairs={{0,1},{1,2},{2,3},{3,4},{4,5},{5,6},{6,7},{7,0},{8,9},{9,10},{10,1... | collective-permute-start | bytes 12344 | tf_op jit(solution)/shard_map/ppermute | solution.py:17
  62.8 5.5 %collective-permute-start.11 = (f32[2,514,1]{1,0,2:T(2,128)S(1)}, f32[2,514,1]{1,0,2:T(2,128)S(1)}, u32[]{:S(2)}, u32[]{:S(2)}) collective-permute-start(f32[2,514,1]{1,0,2:T(2,128)S(1)} %copy.215), channel_id=1, source_target_pairs={{1,0},{2,1},{3,2},{4,3},{5,4},{6,5},{7,6},{0,7},{9,8},{10,9},{11,1... | collective-permute-start | bytes 12344 | tf_op jit(solution)/shard_map/ppermute | solution.py:19
  74.8 5.2 %collective-permute-start.12 = (f32[2,1,512]{2,1,0:T(1,128)S(1)}, f32[2,1,512]{2,1,0:T(1,128)S(1)}, u32[]{:S(2)}, u32[]{:S(2)}) collective-permute-start(f32[2,1,512]{2,1,0:T(1,128)S(1)} %get-tuple-element.84), channel_id=1, source_target_pairs={{0,8},{8,16},{16,24},{24,32},{32,40},{40,48},{48,56},{56,64},{64,7... | collective-permute-start | bytes 12296 | tf_op jit(solution)/shard_map/ppermute | solution.py:17
  80.6 7.3 %collective-permute-start.14 = (f32[2,514,1]{1,0,2:T(2,128)S(1)}, f32[2,514,1]{1,0,2:T(2,128)S(1)}, u32[]{:S(2)}, u32[]{:S(2)}) collective-permute-start(f32[2,514,1]{1,0,2:T(2,128)S(1)} %copy.220), channel_id=1, source_target_pairs={{0,1},{1,2},{2,3},{3,4},{4,5},{5,6},{6,7},{7,0},{8,9},{9,10},{10,1... | collective-permute-start | bytes 12344 | tf_op jit(solution)/shard_map/ppermute | solution.py:17
  83.1 5.4 %collective-permute-start.15 = (f32[2,514,1]{1,0,2:T(2,128)S(1)}, f32[2,514,1]{1,0,2:T(2,128)S(1)}, u32[]{:S(2)}, u32[]{:S(2)}) collective-permute-start(f32[2,514,1]{1,0,2:T(2,128)S(1)} %copy.221), channel_id=1, source_target_pairs={{1,0},{2,1},{3,2},{4,3},{5,4},{6,5},{7,6},{0,7},{9,8},{10,9},{11,1... | collective-permute-start | bytes 12344 | tf_op jit(solution)/shard_map/ppermute | solution.py:19
  95.1 5.2 %collective-permute-start.16 = (f32[2,1,512]{2,1,0:T(1,128)S(1)}, f32[2,1,512]{2,1,0:T(1,128)S(1)}, u32[]{:S(2)}, u32[]{:S(2)}) collective-permute-start(f32[2,1,512]{2,1,0:T(1,128)S(1)} %get-tuple-element.82), channel_id=1, source_target_pairs={{0,8},{8,16},{16,24},{24,32},{32,40},{40,48},{48,56},{56,64},{64,7... | collective-permute-start | bytes 12296 | tf_op jit(solution)/shard_map/ppermute | solution.py:17
  100.8 7.3 %collective-permute-start.18 = (f32[2,514,1]{1,0,2:T(2,128)S(1)}, f32[2,514,1]{1,0,2:T(2,128)S(1)}, u32[]{:S(2)}, u32[]{:S(2)}) collective-permute-start(f32[2,514,1]{1,0,2:T(2,128)S(1)} %copy.226), channel_id=1, source_target_pairs={{0,1},{1,2},{2,3},{3,4},{4,5},{5,6},{6,7},{7,0},{8,9},{9,10},{10,1... | collective-permute-start | bytes 12344 | tf_op jit(solution)/shard_map/ppermute | solution.py:17
  115.7 5.2 %collective-permute-start.20 = (f32[2,1,512]{2,1,0:T(1,128)S(1)}, f32[2,1,512]{2,1,0:T(1,128)S(1)}, u32[]{:S(2)}, u32[]{:S(2)}) collective-permute-start(f32[2,1,512]{2,1,0:T(1,128)S(1)} %get-tuple-element.80), channel_id=1, source_target_pairs={{0,8},{8,16},{16,24},{24,32},{32,40},{40,48},{48,56},{56,64},{64,7... | collective-permute-start | bytes 12296 | tf_op jit(solution)/shard_map/ppermute | solution.py:17
  121.4 7.3 %collective-permute-start.22 = (f32[2,514,1]{1,0,2:T(2,128)S(1)}, f32[2,514,1]{1,0,2:T(2,128)S(1)}, u32[]{:S(2)}, u32[]{:S(2)}) collective-permute-start(f32[2,514,1]{1,0,2:T(2,128)S(1)} %copy.232), channel_id=1, source_target_pairs={{0,1},{1,2},{2,3},{3,4},{4,5},{5,6},{6,7},{7,0},{8,9},{9,10},{10,1... | collective-permute-start | bytes 12344 | tf_op jit(solution)/shard_map/ppermute | solution.py:17
  124.2 5.6 %collective-permute-start.23 = (f32[2,514,1]{1,0,2:T(2,128)S(1)}, f32[2,514,1]{1,0,2:T(2,128)S(1)}, u32[]{:S(2)}, u32[]{:S(2)}) collective-permute-start(f32[2,514,1]{1,0,2:T(2,128)S(1)} %copy.233), channel_id=1, source_target_pairs={{1,0},{2,1},{3,2},{4,3},{5,4},{6,5},{7,6},{0,7},{9,8},{10,9},{11,1... | collective-permute-start | bytes 12344 | tf_op jit(solution)/shard_map/ppermute | solution.py:19
  136.4 5.2 %collective-permute-start.24 = (f32[2,1,512]{2,1,0:T(1,128)S(1)}, f32[2,1,512]{2,1,0:T(1,128)S(1)}, u32[]{:S(2)}, u32[]{:S(2)}) collective-permute-start(f32[2,1,512]{2,1,0:T(1,128)S(1)} %get-tuple-element.78), channel_id=1, source_target_pairs={{0,8},{8,16},{16,24},{24,32},{32,40},{40,48},{48,56},{56,64},{64,7... | collective-permute-start | bytes 12296 | tf_op jit(solution)/shard_map/ppermute | solution.py:17
  142.1 7.3 %collective-permute-start.26 = (f32[2,514,1]{1,0,2:T(2,128)S(1)}, f32[2,514,1]{1,0,2:T(2,128)S(1)}, u32[]{:S(2)}, u32[]{:S(2)}) collective-permute-start(f32[2,514,1]{1,0,2:T(2,128)S(1)} %copy.238), channel_id=1, source_target_pairs={{0,1},{1,2},{2,3},{3,4},{4,5},{5,6},{6,7},{7,0},{8,9},{9,10},{10,1... | collective-permute-start | bytes 12344 | tf_op jit(solution)/shard_map/ppermute | solution.py:17
  158.2 5.2 %collective-permute-start.28 = (f32[2,1,512]{2,1,0:T(1,128)S(1)}, f32[2,1,512]{2,1,0:T(1,128)S(1)}, u32[]{:S(2)}, u32[]{:S(2)}) collective-permute-start(f32[2,1,512]{2,1,0:T(1,128)S(1)} %get-tuple-element.76), channel_id=1, source_target_pairs={{0,8},{8,16},{16,24},{24,32},{32,40},{40,48},{48,56},{56,64},{64,7... | collective-permute-start | bytes 12296 | tf_op jit(solution)/shard_map/ppermute | solution.py:17
  163.9 7.3 %collective-permute-start.30 = (f32[2,514,1]{1,0,2:T(2,128)S(1)}, f32[2,514,1]{1,0,2:T(2,128)S(1)}, u32[]{:S(2)}, u32[]{:S(2)}) collective-permute-start(f32[2,514,1]{1,0,2:T(2,128)S(1)} %copy.244), channel_id=1, source_target_pairs={{0,1},{1,2},{2,3},{3,4},{4,5},{5,6},{6,7},{7,0},{8,9},{9,10},{10,1... | collective-permute-start | bytes 12344 | tf_op jit(solution)/shard_map/ppermute | solution.py:17
  166.7 5.3 %collective-permute-start.31 = (f32[2,514,1]{1,0,2:T(2,128)S(1)}, f32[2,514,1]{1,0,2:T(2,128)S(1)}, u32[]{:S(2)}, u32[]{:S(2)}) collective-permute-start(f32[2,514,1]{1,0,2:T(2,128)S(1)} %copy.245), channel_id=1, source_target_pairs={{1,0},{2,1},{3,2},{4,3},{5,4},{6,5},{7,6},{0,7},{9,8},{10,9},{11,1... | collective-permute-start | bytes 12344 | tf_op jit(solution)/shard_map/ppermute | solution.py:19
  271.8 5.3 %collective-permute-start.32 = (f32[2,1,128]{2,1,0:T(1,128)S(1)}, f32[2,1,128]{2,1,0:T(1,128)S(1)}, u32[]{:S(2)}, u32[]{:S(2)}) collective-permute-start(f32[2,1,128]{2,1,0:T(1,128)S(1)} %get-tuple-element.112), channel_id=1, source_target_pairs={{0,8},{8,16},{16,24},{24,32},{32,40},{40,48},{48,56},{56,64},{64,7... | collective-permute-start | bytes 3080 | tf_op jit(solution)/shard_map/ppermute | solution.py:17
  277.2 8.7 %collective-permute-start.34 = (f32[2,130,1]{2,1,0:T(8,128)S(1)}, f32[2,130,1]{2,1,0:T(8,128)S(1)}, u32[]{:S(2)}, u32[]{:S(2)}) collective-permute-start(f32[2,130,1]{2,1,0:T(8,128)S(1)} %get-tuple-element.110), channel_id=1, source_target_pairs={{0,1},{1,2},{2,3},{3,4},{4,5},{5,6},{6,7},{7,0},{8,9},{9,10},{10,1... | collective-permute-start | bytes 3128 | tf_op jit(solution)/shard_map/ppermute | solution.py:17
  281.5 6.6 %collective-permute-start.35 = (f32[2,130,1]{2,1,0:T(8,128)S(1)}, f32[2,130,1]{2,1,0:T(8,128)S(1)}, u32[]{:S(2)}, u32[]{:S(2)}) collective-permute-start(f32[2,130,1]{2,1,0:T(8,128)S(1)} %get-tuple-element.111), channel_id=1, source_target_pairs={{1,0},{2,1},{3,2},{4,3},{5,4},{6,5},{7,6},{0,7},{9,8},{10,9},{11,1... | collective-permute-start | bytes 3128 | tf_op jit(solution)/shard_map/ppermute | solution.py:19
  (33 other events, 249.6 us)
